TPU v7x, 512 devices: a whole 4x4x16 slice. The times are simulated.
512 devices in a mesh: frame: 16 (over z), dom: 8 (over x, core), coef: 4 (over y).
Axes of the slice: x: 4, y: 4, z: 16, core: 2. Of those that a mesh axis runs over, the one named last changes fastest.
Arguments:
- geometry: float32 [32, 524288], P('coef', ('frame', 'dom')), may hold values from -1 to 1
- fraction: float32 [32, 524288], P('coef', ('frame', 'dom')), may hold values from 0 to 1
- interval: int32 [32, 524288], P('coef', ('frame', 'dom')), may hold values from 0 to 156
- pattern: int32 [32, 4096], P('coef', ('frame', 'dom')), may hold values from 0 to 95
- target: float32 [524288], P(('frame', 'dom')), may hold values from -8 to 8
Outputs:
- solution: float32 [384, 160], P('coef')
- residual: float32 [524288], P(('frame', 'dom'))
Inputs may be any that keep to these rules, and one draw needn't show every extreme that they name: The spline of a slot reads coefficients interval to interval + 3 of its type. Slot s refers to pair type (s // 8) * 96 + pattern.
All inputs are finite; a program needn't handle non-finite values.
Results may differ from a plain program's by a relative error of at most 0.0003.
Values sent between devices are 32-bit elements; how exact they have to be, the bound alone decides.
No kernel may reach another device: no remote copies, remote signals or barrier semaphores. Data moves between devices by JAX's collectives and lax.ppermute only.
A program may use at most 64 MiB of HBM per device.

v0:
```python
import math
import jax
import jax.numpy as jnp
from jax import lax
from jax.sharding import PartitionSpec as P

NK = 160
TYPES = 384
ITERS = 2


def spline_weights(fraction):
    square = fraction * fraction
    cube = square * fraction
    return (
        (1.0 - fraction) ** 3 / 6.0,
        (3.0 * cube - 6.0 * square + 4.0) / 6.0,
        (-3.0 * cube + 3.0 * square + 3.0 * fraction + 1.0) / 6.0,
        cube / 6.0,
    )


def dense_tiles(geom, fraction, interval):
    knots = lax.broadcasted_iota(jnp.int32, (1, NK, 1), 1)
    tiles = jnp.zeros((geom.shape[0], NK, geom.shape[1]), jnp.float32)
    for offset, weight in enumerate(spline_weights(fraction)):
        hit = knots == (interval + offset)[:, None, :]
        tiles = tiles + jnp.where(hit, (geom * weight)[:, None, :], 0.0)
    return tiles


def block_layout(geom):
    tiles_all = geom.shape[1] // 128
    block = math.gcd(8, tiles_all)
    return (block, block * 128, tiles_all // block)


def block_tiles(geometry, fraction, interval, pattern, index, block, width):
    start = index * width
    geom = lax.dynamic_slice_in_dim(geometry, start, width, 1)
    frac = lax.dynamic_slice_in_dim(fraction, start, width, 1)
    knot = lax.dynamic_slice_in_dim(interval, start, width, 1)
    kinds = lax.dynamic_slice_in_dim(pattern, index * block, block, 1)
    tiles = dense_tiles(geom, frac, knot).reshape(geom.shape[0], NK, block, 128)
    return (tiles, kinds, start)


def forward(coeffs, geometry, fraction, interval, pattern):
    block, width, count = block_layout(geometry)

    def forward_step(index, image):
        tiles, kinds, start = block_tiles(
            geometry, fraction, interval, pattern, index, block, width
        )
        chosen = jnp.take(coeffs, kinds, axis=0)
        part = jnp.einsum("sktr,stk->tr", tiles, chosen, precision=lax.Precision.HIGHEST)
        return lax.dynamic_update_slice_in_dim(image, part.reshape(width), start, 0)

    return lax.fori_loop(0, count, forward_step, jnp.zeros((geometry.shape[1],), jnp.float32))


def backward(resid, per_coef, geometry, fraction, interval, pattern):
    block, width, count = block_layout(geometry)
    owners = lax.broadcasted_iota(jnp.int32, (1, 1, per_coef), 2)

    def backward_step(index, total):
        tiles, kinds, start = block_tiles(
            geometry, fraction, interval, pattern, index, block, width
        )
        piece = lax.dynamic_slice_in_dim(resid, start, width, 0).reshape(block, 128)
        contrib = jnp.einsum("sktr,tr->stk", tiles, piece, precision=lax.Precision.HIGHEST)
        picks = (kinds[:, :, None] == owners).astype(jnp.float32)
        return total + jnp.einsum("stc,stk->ck", picks, contrib, precision=lax.Precision.HIGHEST)

    return lax.fori_loop(0, count, backward_step, jnp.zeros((per_coef, NK), jnp.float32))


def on_device(geometry, fraction, interval, pattern, target):
    per_coef = TYPES // lax.axis_size("coef")

    def transpose_sum(resid):
        local = backward(resid, per_coef, geometry, fraction, interval, pattern).reshape(
            per_coef * NK
        )
        share = lax.psum(local, ("frame", "dom"))
        total = lax.psum(jnp.sum(share * share), "coef")
        return (share, total)

    def expand(share):
        return share.reshape(per_coef, NK)

    residual = target
    gradient, gamma = transpose_sum(residual)
    direction = gradient
    solution = jnp.zeros_like(gradient)
    for step_index in range(ITERS):
        partial_image = forward(expand(direction), geometry, fraction, interval, pattern)
        image = lax.psum(partial_image, "coef")
        image_total = lax.psum(jnp.sum(image * image), ("frame", "dom"))
        alpha = gamma / image_total
        solution = solution + alpha * direction
        residual = residual - alpha * image
        if step_index + 1 < ITERS:
            gradient, gamma_next = transpose_sum(residual)
            direction = gradient + gamma_next / gamma * direction
            gamma = gamma_next
    return (expand(solution), residual)


def solution(mesh):
    in_specs = (
        P("coef", ("frame", "dom")),
        P("coef", ("frame", "dom")),
        P("coef", ("frame", "dom")),
        P("coef", ("frame", "dom")),
        P(("frame", "dom")),
    )
    out_specs = (P("coef", None), P(("frame", "dom")))
    return jax.shard_map(
        on_device, mesh=mesh, in_specs=in_specs, out_specs=out_specs, check_vma=False
    )
```

profile of v0, /device:TPU:1, one launch (start us, length us, event | category | flops | bytes accessed | tf_op | source)
XLA Modules:
  0.0 1750.1 jit_solution(9884929640221820795)
XLA Ops:
  0.6 52.4 %while.56 = (s32[]{:T(128)}, f32[96,160]{0,1:T(8,128)S(1)}, s32[8,32]{1,0:T(8,128)}, f32[4096]{0:T(1024)}, s32[8,4096]{1,0:T(8,128)}, /*index=5*/f32[8,4096]{1,0...) while((s32[]{:T(128)}, f32[96,160]{0,1:T(8,128)S(1)}, ...), condition=%wide.region_1.2_spmd.clone, body=%wide.region_0.1_spmd.clone.sunk | while | flops 42192900 | bytes 11854863 | solution.py:75
  5.0 8.4 fusion.118
  18.1 8.4 fusion.118
  31.2 8.4 fusion.118
  44.3 8.4 fusion.118
  53.3 498.0 %psum.56 = f32[15360]{0:T(1024)S(1)} all-reduce(f32[15360]{0:T(1024)S(1)} %reshape.226), channel_id=1, replica_groups=mesh['frame'=16,'dom'=8,'coef'=4] {'frame','dom'}, use_global_device_ids=true, to_apply=%region_2.3 | all-reduce | flops 15360 | bytes 122880 | tf_op jit(solution)/shard_map/psum | solution.py:85
  551.4 53.3 %while.54 = (s32[]{:T(128)}, f32[4096]{0:T(1024)S(1)}, s32[8,4096]{1,0:T(8,128)}, f32[8,4096]{1,0:T(8,128)}, f32[8,4096]{1,0:T(8,128)}, /*index=5*/s32[8,32]{1,0...) while((s32[]{:T(128)}, f32[4096]{0:T(1024)S(1)}, ...), condition=%wide.region_6.0_spmd, body=%wide.region_5.7_spmd.sunk | while | flops 30371208 | bytes 11859845 | solution.py:59
  558.3 6.1 fusion.108
  571.6 6.1 fusion.108
  598.3 6.1 fusion.108
  605.3 14.6 all-reduce
  620.5 256.4 %psum.59 = f32[]{:T(128)} all-reduce(f32[]{:T(128)} %multiply_reduce_fusion.3), channel_id=1, replica_groups=mesh['frame'=16,'dom'=8,'coef'=4] {'frame','dom'}, use_global_device_ids=true, to_apply=%region_9.11 | all-reduce | flops 1 | bytes 8 | tf_op jit(solution)/shard_map/psum | solution.py:99
  878.3 49.7 %while.57 = (s32[]{:T(128)}, f32[96,160]{0,1:T(8,128)S(1)}, s32[8,32]{1,0:T(8,128)}, f32[4096]{0:T(1024)S(1)}, s32[8,4096]{1,0:T(8,128)}, /*index=5*/f32[8,4096]...) while((s32[]{:T(128)}, f32[96,160]{0,1:T(8,128)S(1)}, ...), condition=%wide.region_11.13_spmd.clone, body=%wide.region_10.12_spmd.clone.sunk | while | flops 42192900 | bytes 11854863 | solution.py:75
  882.0 8.4 fusion.124
  894.4 8.4 fusion.124
  906.9 8.4 fusion.124
  919.3 8.4 fusion.124
  928.3 485.9 %psum.60 = f32[15360]{0:T(1024)S(1)} all-reduce(f32[15360]{0:T(1024)S(1)} %reshape.228), channel_id=1, replica_groups=mesh['frame'=16,'dom'=8,'coef'=4] {'frame','dom'}, use_global_device_ids=true, to_apply=%region_12.14 | all-reduce | flops 15360 | bytes 122880 | tf_op jit(solution)/shard_map/psum | solution.py:85
  1414.8 6.9 psum.61
  1423.1 53.3 %while.55 = (s32[]{:T(128)}, f32[4096]{0:T(1024)S(1)}, s32[8,4096]{1,0:T(8,128)}, f32[8,4096]{1,0:T(8,128)}, f32[8,4096]{1,0:T(8,128)}, /*index=5*/s32[8,32]{1,0...) while((s32[]{:T(128)}, f32[4096]{0:T(1024)S(1)}, ...), condition=%wide.region_16.18_spmd, body=%wide.region_15.17_spmd.sunk | while | flops 30371208 | bytes 11859845 | solution.py:59
  1430.0 6.1 fusion.113
  1456.6 6.1 fusion.113
  1476.4 12.1 psum.62
  1489.1 258.2 %psum.63 = f32[]{:T(128)} all-reduce(f32[]{:T(128)} %multiply_reduce_fusion.2), channel_id=1, replica_groups=mesh['frame'=16,'dom'=8,'coef'=4] {'frame','dom'}, use_global_device_ids=true, to_apply=%region_19.21 | all-reduce | flops 1 | bytes 8 | tf_op jit(solution)/shard_map/psum | solution.py:99
  (305 shorter events, 114.0 us)
Async XLA Ops:
  4.3 9.1 copy-start
  17.4 9.1 copy-start
  30.5 9.1 copy-start
  43.6 9.1 copy-start
  551.4 326.9 %copy-start.4 = (f32[4096]{0:T(1024)S(1)}, f32[4096]{0:T(1024)}, u32[]{:S(2)}) copy-start(f32[4096]{0:T(1024)} %get-tuple-element.1094) | copy-start | bytes 49156
  551.4 6.0 copy-start.1
  564.8 6.0 copy-start.1
  578.1 6.0 copy-start.1
  591.4 6.0 copy-start.1
  882.0 8.4 copy-start.2
  894.4 8.4 copy-start.2
  906.8 8.4 copy-start.2
  919.3 8.4 copy-start.2
  1423.1 6.0 copy-start.3
  1436.4 6.0 copy-start.3
  1449.8 6.0 copy-start.3
  1463.1 6.0 copy-start.3
where the time goes:
time: 1750 us
  blocking collectives  1530 us (87%)
  matrix products  118 us (7%)
  other arithmetic  78.9 us (5%)
    psum x2, blocking collectives, transpose_sum(): share = lax.psum(local, ('frame', 'dom'))  984 us
    psum x2, blocking collectives, on_device(): image_total = lax.psum(jnp.sum(image * image), ('frame', 'dom'))  515 us
    dot_general x8, matrix products, backward_step(): jnp.einsum('sktr,tr->stk', tiles, piece, precision=lax.Precision.HIGHEST)  66.9 us
    add x16, other arithmetic, dense_tiles(): tiles = tiles + jnp.where(hit, (geom * weight)[:, None, :], 0.0)  49.2 us
    dot_general x8, matrix products, forward_step(): jnp.einsum('sktr,stk->tr', tiles, chosen, precision=lax.Precision.HIGHEST)  49 us

commit v1 on v0

--- a/solution.py
+++ b/solution.py
@@ -82,7 +82,7 @@
         local = backward(resid, per_coef, geometry, fraction, interval, pattern).reshape(
             per_coef * NK
         )
-        share = lax.psum(local, ("frame", "dom"))
+        share = lax.psum(lax.psum(local, "dom"), "frame")
         total = lax.psum(jnp.sum(share * share), "coef")
         return (share, total)
 

time: 1750 us -> 925 us (0.53)
  blocking collectives: 1530 us -> 704 us
    psum x2 -> x4, blocking collectives: 984 us -> 133 us  [transpose_sum(): share = lax.psum(lax.psum(local, 'dom'), 'frame')]
    psum x2, blocking collectives: 515 us -> 538 us  [on_device(): image_total = lax.psum(jnp.sum(image * image), ('frame', 'dom'))]
where the time goes in v1:
time: 925 us; the launch traced here: 922 us
  blocking collectives  704 us (76%)
  matrix products  118 us (13%)
  other arithmetic  78.9 us (9%)
  local copies, waits for them, and re-layouts  14.3 us (2%)
    psum x2, blocking collectives, on_device(): image_total = lax.psum(jnp.sum(image * image), ('frame', 'dom'))  538 us
    psum x4, blocking collectives, transpose_sum(): share = lax.psum(lax.psum(local, 'dom'), 'frame')  133 us
    dot_general x8, matrix products, backward_step(): jnp.einsum('sktr,tr->stk', tiles, piece, precision=lax.Precision.HIGHEST)  66.9 us
    add x16, other arithmetic, dense_tiles(): tiles = tiles + jnp.where(hit, (geom * weight)[:, None, :], 0.0)  49.2 us
    dot_general x8, matrix products, forward_step(): jnp.einsum('sktr,stk->tr', tiles, chosen, precision=lax.Precision.HIGHEST)  49 us
    psum x2, blocking collectives, on_device(): image = lax.psum(partial_image, 'coef')  26.7 us

profile of v1, /device:TPU:1, one launch (start us, length us, event | category | flops | bytes accessed | tf_op | source)
XLA Modules:
  0.0 922.1 jit_solution(2606078066554333685)
XLA Ops:
  0.6 52.4 %while.56 = (s32[]{:T(128)}, f32[96,160]{0,1:T(8,128)S(1)}, s32[8,32]{1,0:T(8,128)}, f32[4096]{0:T(1024)}, s32[8,4096]{1,0:T(8,128)}, /*index=5*/f32[8,4096]{1,0...) while((s32[]{:T(128)}, f32[96,160]{0,1:T(8,128)S(1)}, ...), condition=%wide.region_1.2_spmd.clone, body=%wide.region_0.1_spmd.clone.sunk | while | flops 42192900 | bytes 11854863 | solution.py:75
  5.0 8.4 fusion.118
  18.1 8.4 fusion.118
  31.2 8.4 fusion.118
  44.3 8.4 fusion.118
  53.3 27.7 %psum.70 = f32[15360]{0:T(1024)S(1)} all-reduce(f32[15360]{0:T(1024)S(1)} %reshape.226), channel_id=1, replica_groups=mesh['frame'=16,'dom'=8,'coef'=4] {'dom'}, use_global_device_ids=true, to_apply=%region_2.3 | all-reduce | flops 15360 | bytes 122880 | tf_op jit(solution)/shard_map/psum | solution.py:85
  80.9 44.6 %psum.71 = f32[15360]{0:T(1024)S(1)} all-reduce(f32[15360]{0:T(1024)S(1)} %psum.70), channel_id=1, replica_groups=mesh['frame'=16,'dom'=8,'coef'=4] {'frame'}, use_global_device_ids=true, to_apply=%region_3.4 | all-reduce | flops 15360 | bytes 122880 | tf_op jit(solution)/shard_map/psum | solution.py:85
  125.6 53.3 %while.54 = (s32[]{:T(128)}, f32[4096]{0:T(1024)S(1)}, s32[8,4096]{1,0:T(8,128)}, f32[8,4096]{1,0:T(8,128)}, f32[8,4096]{1,0:T(8,128)}, /*index=5*/s32[8,32]{1,0...) while((s32[]{:T(128)}, f32[4096]{0:T(1024)S(1)}, ...), condition=%wide.region_7.0_spmd, body=%wide.region_6.8_spmd.sunk | while | flops 30371208 | bytes 11859845 | solution.py:59
  132.5 6.1 fusion.108
  145.8 6.1 fusion.108
  172.5 6.1 fusion.108
  179.5 14.6 %all-reduce = (f32[4096]{0:T(1024)S(1)}, f32[]{:T(128)}) all-reduce(f32[4096]{0:T(1024)S(1)} %get-tuple-element.530, f32[]{:T(128)} %multiply_reduce_fusion.1), channel_id=1, replica_groups=mesh['frame'=16,'dom'=8,'coef'=4] {'coef'}, use_global_device_ids=true, to_apply=%region_8.10 | all-reduce | flops 4097 | bytes 32776 | tf_op jit(solution)/shard_map/psum | solution.py:98
  194.7 268.3 %psum.74 = f32[]{:T(128)} all-reduce(f32[]{:T(128)} %multiply_reduce_fusion.3), channel_id=1, replica_groups=mesh['frame'=16,'dom'=8,'coef'=4] {'frame','dom'}, use_global_device_ids=true, to_apply=%region_10.12 | all-reduce | flops 1 | bytes 8 | tf_op jit(solution)/shard_map/psum | solution.py:99
  464.4 49.7 %while.57 = (s32[]{:T(128)}, f32[96,160]{0,1:T(8,128)S(1)}, s32[8,32]{1,0:T(8,128)}, f32[4096]{0:T(1024)S(1)}, s32[8,4096]{1,0:T(8,128)}, /*index=5*/f32[8,4096]...) while((s32[]{:T(128)}, f32[96,160]{0,1:T(8,128)S(1)}, ...), condition=%wide.region_12.14_spmd.clone, body=%wide.region_11.13_spmd.clone.sunk | while | flops 42192900 | bytes 11854863 | solution.py:75
  468.1 8.4 fusion.124
  480.5 8.4 fusion.124
  492.9 8.4 fusion.124
  505.4 8.4 fusion.124
  514.3 21.5 %psum.75 = f32[15360]{0:T(1024)S(1)} all-reduce(f32[15360]{0:T(1024)S(1)} %reshape.228), channel_id=1, replica_groups=mesh['frame'=16,'dom'=8,'coef'=4] {'dom'}, use_global_device_ids=true, to_apply=%region_13.15 | all-reduce | flops 15360 | bytes 122880 | tf_op jit(solution)/shard_map/psum | solution.py:85
  535.8 39.0 %psum.76 = f32[15360]{0:T(1024)S(1)} all-reduce(f32[15360]{0:T(1024)S(1)} %psum.75), channel_id=1, replica_groups=mesh['frame'=16,'dom'=8,'coef'=4] {'frame'}, use_global_device_ids=true, to_apply=%region_14.16 | all-reduce | flops 15360 | bytes 122880 | tf_op jit(solution)/shard_map/psum | solution.py:85
  575.4 7.2 psum.77
  584.0 53.3 %while.55 = (s32[]{:T(128)}, f32[4096]{0:T(1024)S(1)}, s32[8,4096]{1,0:T(8,128)}, f32[8,4096]{1,0:T(8,128)}, f32[8,4096]{1,0:T(8,128)}, /*index=5*/s32[8,32]{1,0...) while((s32[]{:T(128)}, f32[4096]{0:T(1024)S(1)}, ...), condition=%wide.region_18.20_spmd, body=%wide.region_17.19_spmd.sunk | while | flops 30371208 | bytes 11859845 | solution.py:59
  637.3 12.1 %psum.78 = f32[4096]{0:T(1024)S(1)} all-reduce(f32[4096]{0:T(1024)S(1)} %get-tuple-element.532), channel_id=1, replica_groups=mesh['frame'=16,'dom'=8,'coef'=4] {'coef'}, use_global_device_ids=true, to_apply=%region_19.21 | all-reduce | flops 4096 | bytes 32768 | tf_op jit(solution)/shard_map/psum | solution.py:98
  650.0 269.3 %psum.79 = f32[]{:T(128)} all-reduce(f32[]{:T(128)} %multiply_reduce_fusion.2), channel_id=1, replica_groups=mesh['frame'=16,'dom'=8,'coef'=4] {'frame','dom'}, use_global_device_ids=true, to_apply=%region_21.23 | all-reduce | flops 1 | bytes 8 | tf_op jit(solution)/shard_map/psum | solution.py:99
  (307 shorter events, 126.2 us)
Async XLA Ops:
  4.3 9.1 copy-start
  17.4 9.1 copy-start
  30.5 9.1 copy-start
  43.6 9.1 copy-start
  125.6 338.8 %copy-start.4 = (f32[4096]{0:T(1024)S(1)}, f32[4096]{0:T(1024)}, u32[]{:S(2)}) copy-start(f32[4096]{0:T(1024)} %get-tuple-element.1094) | copy-start | bytes 49156
  125.6 6.0 copy-start.1
  139.0 6.0 copy-start.1
  152.3 6.0 copy-start.1
  165.6 6.0 copy-start.1
  468.1 8.4 copy-start.2
  480.5 8.4 copy-start.2
  492.9 8.4 copy-start.2
  505.3 8.4 copy-start.2
  584.0 6.0 copy-start.3
  597.4 6.0 copy-start.3
  610.7 6.0 copy-start.3
  624.0 6.0 copy-start.3

commit v2 on v0

--- a/solution.py
+++ b/solution.py
@@ -82,7 +82,7 @@
         local = backward(resid, per_coef, geometry, fraction, interval, pattern).reshape(
             per_coef * NK
         )
-        share = lax.psum(local, ("frame", "dom"))
+        share = jnp.sum(lax.all_gather(local, ("frame", "dom")), axis=0)
         total = lax.psum(jnp.sum(share * share), "coef")
         return (share, total)
 

time: 1750 us -> 1060 us (0.61)
  blocking collectives: 1530 us -> 538 us
  waiting for transfers between devices: 0 us -> 290 us
    psum x2 -> x0, blocking collectives: 984 us -> none  [transpose_sum(): share = lax.psum(local, ('frame', 'dom'))]
    all_gather x0 -> x2, waiting for transfers between devices: none -> 290 us  [transpose_sum(): share = jnp.sum(lax.all_gather(local, ('frame', 'dom')), axis=0)]
  transfers between devices with their start and end apart: 0 -> 2, of which waited for: 0 -> 2; matrix products, arithmetic and copies ran while one was open for 0% -> 0% of each run, Pallas kernels for 0% -> 0%
where the time goes in v2:
time: 1060 us
  blocking collectives  538 us (51%)
  waiting for transfers between devices  290 us (27%)
  matrix products  118 us (11%)
  other arithmetic  73.3 us (7%)
  between operations  18.1 us (2%)
  local copies, waits for them, and re-layouts  15.5 us (1%)
    psum x2, blocking collectives, on_device(): image_total = lax.psum(jnp.sum(image * image), ('frame', 'dom'))  504 us
    all_gather x2, waiting for transfers between devices, transpose_sum(): share = jnp.sum(lax.all_gather(local, ('frame', 'dom')), axis=0)  290 us
    dot_general x8, matrix products, backward_step(): jnp.einsum('sktr,tr->stk', tiles, piece, precision=lax.Precision.HIGHEST)  66.9 us
    add x16, other arithmetic, dense_tiles(): tiles = tiles + jnp.where(hit, (geom * weight)[:, None, :], 0.0)  49.2 us
    dot_general x8, matrix products, forward_step(): jnp.einsum('sktr,stk->tr', tiles, chosen, precision=lax.Precision.HIGHEST)  49 us
    psum x2, blocking collectives, on_device(): image = lax.psum(partial_image, 'coef')  25.2 us
  transfers between devices with their start and end apart: 2, of which 2 were waited for; matrix products, arithmetic and copies ran while one was open for 0% of the time, Pallas kernels for 0%

profile of v2, /device:TPU:1, one launch (start us, length us, event | category | flops | bytes accessed | tf_op | source)
XLA Modules:
  0.0 1055.5 jit_solution(6792258564208977422)
XLA Ops:
  7.2 52.4 %while.56 = (s32[]{:T(128)}, f32[96,160]{0,1:T(8,128)S(1)}, s32[8,32]{1,0:T(8,128)}, f32[4096]{0:T(1024)}, s32[8,4096]{1,0:T(8,128)}, /*index=5*/f32[8,4096]{1,0...) while((s32[]{:T(128)}, f32[96,160]{0,1:T(8,128)S(1)}, ...), condition=%wide.region_1.2_spmd.clone, body=%wide.region_0.1_spmd.clone.sunk | while | flops 42192900 | bytes 11854863 | solution.py:75
  11.6 8.4 fusion.118
  24.7 8.4 fusion.118
  37.8 8.4 fusion.118
  50.9 8.4 fusion.118
  60.8 151.3 %all-gather.5.cloned.1.call-done = f32[128,1,15360]{2,1,0:T(1,128)} async-done(((f32[1,1,15360]{2,1,0:T(1,128)}), f32[128,1,15360]{2,1,0:T(1,128)}) %all-gather.5.cloned.1.call-update) | async-done | bytes 7864336 | tf_op jit(solution)/shard_map/all_gather | solution.py:85
  212.1 6.4 reduce_sum.56
  219.2 47.1 %while.54 = (s32[]{:T(128)}, f32[4096]{0:T(1024)S(1)}, s32[8,4096]{1,0:T(8,128)S(1)}, f32[8,4096]{1,0:T(8,128)S(1)}, f32[8,4096]{1,0:T(8,128)S(1)}, /*index=5*/s...) while((s32[]{:T(128)}, f32[4096]{0:T(1024)S(1)}, ...), condition=%wide.region_6.0_spmd, body=%wide.region_5.7_spmd.sunk | while | flops 30371208 | bytes 11855721 | solution.py:59
  224.6 6.1 fusion.108
  236.4 6.1 fusion.108
  248.2 6.1 fusion.108
  266.4 14.4 %all-reduce = (f32[4096]{0:T(1024)S(1)}, f32[]{:T(128)}) all-reduce(f32[4096]{0:T(1024)S(1)} %get-tuple-element.530, f32[]{:T(128)} %multiply_reduce_fusion.1), channel_id=1, replica_groups=mesh['frame'=16,'dom'=8,'coef'=4] {'coef'}, use_global_device_ids=true, to_apply=%region_7.9 | all-reduce | flops 4097 | bytes 32776 | tf_op jit(solution)/shard_map/psum | solution.py:98
  281.4 251.0 %psum.44 = f32[]{:T(128)} all-reduce(f32[]{:T(128)} %multiply_reduce_fusion.3), channel_id=1, replica_groups=mesh['frame'=16,'dom'=8,'coef'=4] {'frame','dom'}, use_global_device_ids=true, to_apply=%region_9.11 | all-reduce | flops 1 | bytes 8 | tf_op jit(solution)/shard_map/psum | solution.py:99
  533.8 43.6 %while.57 = (s32[]{:T(128)}, f32[96,160]{0,1:T(8,128)S(1)}, s32[8,32]{1,0:T(8,128)S(1)}, f32[4096]{0:T(1024)S(1)}, s32[8,4096]{1,0:T(8,128)S(1)}, /*index=5*/f32...) while((s32[]{:T(128)}, f32[96,160]{0,1:T(8,128)S(1)}, ...), condition=%wide.region_11.13_spmd.clone, body=%wide.region_10.12_spmd.clone.sunk | while | flops 42192900 | bytes 11850739 | solution.py:75
  535.9 8.4 fusion.124
  546.8 8.4 fusion.124
  557.7 8.4 fusion.124
  568.6 8.4 fusion.124
  578.2 138.8 %all-gather.7.cloned.1.call-done = f32[128,1,15360]{2,1,0:T(1,128)} async-done(((f32[1,1,15360]{2,1,0:T(1,128)}), f32[128,1,15360]{2,1,0:T(1,128)}) %all-gather.7.cloned.1.call-update) | async-done | bytes 7864336 | tf_op jit(solution)/shard_map/all_gather | solution.py:85
  717.1 6.4 reduce_sum.59
  724.2 9.4 psum.45
  734.9 47.1 %while.55 = (s32[]{:T(128)}, f32[4096]{0:T(1024)S(1)}, s32[8,4096]{1,0:T(8,128)S(1)}, f32[8,4096]{1,0:T(8,128)S(1)}, f32[8,4096]{1,0:T(8,128)S(1)}, /*index=5*/s...) while((s32[]{:T(128)}, f32[4096]{0:T(1024)S(1)}, ...), condition=%wide.region_16.18_spmd, body=%wide.region_15.17_spmd.sunk | while | flops 30371208 | bytes 11855721 | solution.py:59
  782.0 10.8 %psum.46 = f32[4096]{0:T(1024)S(1)} all-reduce(f32[4096]{0:T(1024)S(1)} %get-tuple-element.532), channel_id=1, replica_groups=mesh['frame'=16,'dom'=8,'coef'=4] {'coef'}, use_global_device_ids=true, to_apply=%region_17.19 | all-reduce | flops 4096 | bytes 32768 | tf_op jit(solution)/shard_map/psum | solution.py:98
  793.4 252.5 %psum.47 = f32[]{:T(128)} all-reduce(f32[]{:T(128)} %multiply_reduce_fusion.2), channel_id=1, replica_groups=mesh['frame'=16,'dom'=8,'coef'=4] {'frame','dom'}, use_global_device_ids=true, to_apply=%region_19.21 | all-reduce | flops 1 | bytes 8 | tf_op jit(solution)/shard_map/psum | solution.py:99
  (294 shorter events, 109.3 us)
Async XLA Ops:
  7.2 205.0 %all-gather.5.cloned.1.call-start = ((), (), s32[]{:S(2)}) async-start(), calls=%async_computation | async-start | bytes 7925760 | tf_op jit(solution)/shard_map/all_gather | solution.py:85
  10.9 9.1 copy-start.3
  24.0 9.1 copy-start.3
  37.1 9.1 copy-start.3
  50.2 9.1 copy-start.3
  59.7 159.6 %copy-start = (s32[8,4096]{1,0:T(8,128)S(1)}, s32[8,4096]{1,0:T(8,128)}, u32[]{:S(2)}) copy-start(s32[8,4096]{1,0:T(8,128)} %get-tuple-element.1103) | copy-start | bytes 393220
  59.7 159.6 %copy-start.1 = (f32[8,4096]{1,0:T(8,128)S(1)}, f32[8,4096]{1,0:T(8,128)}, u32[]{:S(2)}) copy-start(f32[8,4096]{1,0:T(8,128)} %get-tuple-element.1106) | copy-start | bytes 393220
  59.7 159.5 %copy-start.2 = (f32[8,4096]{1,0:T(8,128)S(1)}, f32[8,4096]{1,0:T(8,128)}, u32[]{:S(2)}) copy-start(f32[8,4096]{1,0:T(8,128)} %get-tuple-element.1109) | copy-start | bytes 393220
  59.7 159.5 %copy-start.4 = (s32[8,32]{1,0:T(8,128)S(1)}, s32[8,32]{1,0:T(8,128)}, u32[]{:S(2)}) copy-start(s32[8,32]{1,0:T(8,128)} %get-tuple-element.1112) | copy-start | bytes 3076
  60.6 656.5 %all-gather.7.cloned.1.call-start = ((), (), s32[]{:S(2)}) async-start(), calls=%async_computation.1 | async-start | bytes 7925760 | tf_op jit(solution)/shard_map/all_gather | solution.py:85
  219.2 314.5 %copy-start.5 = (f32[4096]{0:T(1024)S(1)}, f32[4096]{0:T(1024)}, u32[]{:S(2)}) copy-start(f32[4096]{0:T(1024)} %get-tuple-element.1120) | copy-start | bytes 49156
Sparse Core Ops, SparseCore 0:
  60.7 151.3 all-gather.4
  578.4 138.6 all-gather.6
